TPU v7x, 32 devices: a whole 2x2x4 slice. The times are simulated.
32 devices in a mesh: wa: 4 (over z), vert: 8 (over y, x, core).
Axes of the slice: x: 2, y: 2, z: 4, core: 2. Of those that a mesh axis runs over, the one named last changes fastest.
Arguments:
- hidden_in: bfloat16 [384, 8192], P(None, 'wa')
- gate_levels: bfloat16 [8192, 28672], P('wa', 'vert'), may hold values from -127 to 127, as said below
- up_levels: bfloat16 [8192, 28672], P('wa', 'vert'), may hold values from -127 to 127, as said below
- gate_scale: float32 [28672], P('vert'), as said below
- up_scale: float32 [28672], P('vert'), as said below
- down_levels: bfloat16 [28672, 8192], P('vert', 'wa'), may hold values from -127 to 127, as said below
- down_scale: float32 [8192], P('wa'), as said below
- norm_gain: float32 [8192], P('wa'), may hold values from 0.5 to 1.5
- head_weight: bfloat16 [8192, 16000], P('wa', 'vert')
- reward_states: bfloat16 [4, 384, 4096], P('wa', None, 'vert'), may hold values from -6 to 6
- reward_gain: float32 [4, 4096], P('wa'), may hold values from 0.5 to 1.5
- reward_heads: bfloat16 [4, 4096, 16000], P('wa', None, 'vert')
- preference: int32 [384, 4], P(None, 'wa'), may hold values from 0 to 16
- token_ids: int32 [384], P('wa'), may hold values from 0 to 15999
Outputs:
- log_probs: float32 [384, 16000], P('wa', 'vert')
- chosen: float32 [384], P('wa')
Inputs may be any that keep to these rules, and one draw needn't show every extreme that they name: `gate_levels`: whole numbers. `up_levels`: whole numbers. `down_levels`: whole numbers. `gate_scale`: positive. `up_scale`: positive. `down_scale`: positive.
All inputs are finite; a program needn't handle non-finite values.
Results may differ from a plain program's by a relative error of at most 0.0025.
Values may be sent and summed in bfloat16 or wider, within the bound.
A program may use at most 128 MiB of HBM per device.

v0:
```python
import jax
import jax.numpy as jnp
from jax import lax
from jax.sharding import PartitionSpec as P

D = 8192


def log_total(values):
    local_top = jnp.max(values, axis=-1)
    top = lax.pmax(local_top, "vert")
    total = lax.psum(jnp.sum(jnp.exp(values - top[..., None]), axis=-1), "vert")
    return top + jnp.log(total)


def normalize(resid, norm_gain):
    squares = lax.psum(jnp.sum(resid * resid, axis=1), "wa")
    return (resid * lax.rsqrt(squares[:, None] / D + 1e-05) * norm_gain).astype(jnp.bfloat16)


def local(
    hidden_in,
    gate_levels,
    up_levels,
    gate_scale,
    up_scale,
    down_levels,
    down_scale,
    norm_gain,
    head_weight,
    reward_states,
    reward_gain,
    reward_heads,
    preference,
    token_ids,
):
    gate_part = jnp.dot(hidden_in, gate_levels, preferred_element_type=jnp.float32)
    up_part = jnp.dot(hidden_in, up_levels, preferred_element_type=jnp.float32)
    gate_share, up_share = (
        lax.psum_scatter(gate_part, "wa", scatter_dimension=0, tiled=True),
        lax.psum_scatter(up_part, "wa", scatter_dimension=0, tiled=True),
    )
    hidden_share = (jax.nn.silu(gate_share * gate_scale) * (up_share * up_scale)).astype(
        jnp.bfloat16
    )
    down_part = jnp.dot(
        lax.all_gather(hidden_share, "wa", axis=0, tiled=True),
        down_levels,
        preferred_element_type=jnp.float32,
    )
    down = lax.psum(down_part, "vert") * down_scale
    resid = hidden_in.astype(jnp.float32) + down
    normed = normalize(resid, norm_gain)
    base_part = jnp.dot(normed, head_weight, preferred_element_type=jnp.float32)
    states = lax.all_gather(reward_states, "vert", axis=2, tiled=True)
    state_values = states.astype(jnp.float32)
    state_scale = lax.rsqrt(jnp.mean(state_values * state_values, axis=2, keepdims=True) + 1e-05)
    reward_normed = (state_values * state_scale * reward_gain[:, None, :]).astype(jnp.bfloat16)
    reward_logits = jnp.einsum(
        "rnd,rdv->rnv", reward_normed, reward_heads, preferred_element_type=jnp.float32
    )
    reward_logp = reward_logits - log_total(reward_logits)[..., None]
    weights = preference.astype(jnp.float32).T / 16.0
    weighted = jnp.sum(weights[:, :, None] * reward_logp, axis=0)
    base_rows, reward_rows = (
        lax.psum_scatter(base_part, "wa", scatter_dimension=0, tiled=True),
        lax.psum_scatter(weighted, "wa", scatter_dimension=0, tiled=True),
    )
    base_logp = base_rows - log_total(base_rows)[:, None]
    mix = base_logp + reward_rows
    log_probs = mix - log_total(mix)[:, None]
    columns = log_probs.shape[1]
    vocab_index = lax.axis_index("vert") * columns + lax.iota(jnp.int32, columns)
    picked = jnp.sum(jnp.where(vocab_index[None, :] == token_ids[:, None], log_probs, 0.0), axis=1)
    chosen = lax.psum(picked, "vert")
    return (log_probs, chosen)


def solution(mesh):
    return jax.shard_map(
        local,
        mesh=mesh,
        in_specs=(
            P(None, "wa"),
            P("wa", "vert"),
            P("wa", "vert"),
            P("vert"),
            P("vert"),
            P("vert", "wa"),
            P("wa"),
            P("wa"),
            P("wa", "vert"),
            P("wa", None, "vert"),
            P("wa", None),
            P("wa", None, "vert"),
            P(None, "wa"),
            P("wa"),
        ),
        out_specs=(P("wa", "vert"), P("wa")),
        check_vma=False,
    )
```

profile of v0, /device:TPU:9, one launch (start us, length us, event | category | flops | bytes accessed | tf_op | source)
XLA Modules:
  0.0 598.4 jit_solution(16149824593378037764)
XLA Ops:
  7.2 11.1 %fusion.16 = f32[384,3584]{1,0:T(8,128)} fusion(bf16[384,2048]{1,0:T(8,128)(2,1)} %param.14, bf16[2048,3584]{1,0:T(8,128)(2,1)} %param.16), kind=kOutput, calls=%fused_computation.35 | convolution fusion | flops 5637144576 | bytes 21757952 | tf_op jit(solution)/shard_map/dot_general | solution.py:38
  19.7 11.6 %fusion.15 = f32[384,3584]{1,0:T(8,128)} fusion(bf16[384,2048]{1,0:T(8,128)(2,1)S(1)} %copy-done.3, bf16[2048,3584]{1,0:T(8,128)(2,1)} %param.15), kind=kOutput, calls=%fused_computation.34 | convolution fusion | flops 5637144576 | bytes 21757952 | tf_op jit(solution)/shard_map/dot_general | solution.py:37
  31.4 86.3 %reduce-scatter.11.cloned.1.call-done = f32[96,3584]{1,0:T(8,128)} async-done(((f32[384,3584]{1,0:T(8,128)}), f32[96,3584]{1,0:T(8,128)}) %reduce-scatter.11.cloned.1.call-update) | async-done | bytes 1376272 | tf_op jit(solution)/shard_map/reduce_scatter | solution.py:41
  117.6 100.9 %reduce-scatter.9.cloned.1.call-done = f32[96,3584]{1,0:T(8,128)} async-done(((f32[384,3584]{1,0:T(8,128)}), f32[96,3584]{1,0:T(8,128)}) %reduce-scatter.9.cloned.1.call-update) | async-done | bytes 1376272 | tf_op jit(solution)/shard_map/reduce_scatter | solution.py:40
  218.5 3.0 multiply_convert_fusion.2
  221.6 55.3 %all-gather.3.cloned.1.call-done = bf16[384,3584]{1,0:T(8,128)(2,1)} async-done(((bf16[96,3584]{1,0:T(8,128)(2,1)}), bf16[384,3584]{1,0:T(8,128)(2,1)}) %all-gather.3.cloned.1.call-update) | async-done | bytes 2752528 | tf_op jit(solution)/shard_map/all_gather | solution.py:47
  276.9 11.0 %fusion.17 = f32[384,2048]{1,0:T(8,128)} fusion(bf16[384,3584]{1,0:T(8,128)(2,1)} %all-gather.3.cloned.1.call-done, bf16[3584,2048]{1,0:T(8,128)(2,1)} %param.19), kind=kOutput, calls=%fused_computation.36 | convolution fusion | flops 5637144576 | bytes 20578304 | tf_op jit(solution)/shard_map/dot_general | solution.py:46
  288.6 69.7 %all-reduce.4.cloned.1.call-done = f32[384,2048]{1,0:T(8,128)} async-done(((f32[384,2048]{1,0:T(8,128)}), f32[384,2048]{1,0:T(8,128)}) %all-reduce.4.cloned.1.call-update) | async-done | bytes 3145744 | tf_op jit(solution)/shard_map/psum | solution.py:51
  358.3 3.1 multiply_reduce_fusion
  361.4 6.9 %psum.43 = f32[384]{0:T(512)S(1)} all-reduce(f32[384]{0:T(512)S(1)} %multiply_reduce_fusion), channel_id=1, replica_groups=mesh['wa'=4,'vert'=8] {'wa'}, use_global_device_ids=true, to_apply=%region_4.5 | all-reduce | flops 384 | bytes 3072 | tf_op jit(solution)/shard_map/psum | solution.py:17
  368.3 9.1 %fusion.9 = f32[384,2000]{1,0:T(8,128)} fusion(bf16[2048,2000]{0,1:T(8,128)(2,1)} %param.22, f32[384,2048]{1,0:T(8,128)S(1)} %copy-done.2, bf16[384,2048]{1,0:T(8,128)(2,1)} %param.14, f32[2048]{0:T(1024)S(1)} %copy-done.10, f32[384]{0:T(512)S(1)} %add_rsqrt_fusion.1, f32[2048]{0:T(1024)S(1)} %copy-done.6), kind=kOutput, calls=%fused_computation.15 | convolution fusion | flops 3150446592 | bytes 16000512
  378.1 15.4 %all-gather.5.cloned.1.call-done = bf16[1,384,4096]{2,1,0:T(8,128)(2,1)} async-done(((bf16[1,384,512]{2,1,0:T(8,128)(2,1)}), bf16[1,384,4096]{2,1,0:T(8,128)(2,1)}) %all-gather.5.cloned.1.call-update) | async-done | bytes 3145744 | tf_op jit(solution)/shard_map/all_gather | solution.py:55
  393.4 2.7 fusion.2
  396.3 12.0 %fusion.14 = (f32[384]{0:T(512)S(1)}, f32[384,2000]{0,1:T(8,128)S(1)}) fusion(bf16[1,4096,2000]{1,2,0:T(8,128)(2,1)} %param.25, bf16[1,384,4096]{2,1,0:T(8,128)(2,1)S(1)} %copy-done.1, f32[4096]{0:T(1024)S(1)} %bitcast.20, f32[384]{0:T(512)S(1)} %add_rsqrt_fusion), kind=kOutput, calls=%fused_computation.33 | convolution fusion | flops 6298514944 | bytes 22621184 | tf_op jit(solution)/shard_map/rnd,rdv->rnv/dot_general | solution.py:59
  408.3 46.6 %reduce-scatter.13.cloned.1.call-done = f32[96,2000]{1,0:T(8,128)} async-done(((f32[384,2000]{1,0:T(8,128)}), f32[96,2000]{1,0:T(8,128)}) %reduce-scatter.13.cloned.1.call-update) | async-done | bytes 768016
  456.2 11.9 %all-reduce.1 = (f32[1,384]{1,0:T(1,128)S(1)}, f32[96]{0:T(128)S(1)}) all-reduce(f32[1,384]{1,0:T(1,128)S(1)} %reduce_max.31, f32[96]{0:T(128)S(1)} %reduce_max.29), channel_id=1, replica_groups=mesh['wa'=4,'vert'=8] {'vert'}, use_global_device_ids=true, to_apply=%region_12.13 | all-reduce | flops 480 | bytes 3840 | tf_op jit(solution)/shard_map/pmax | solution.py:11
  468.7 2.5 copy.23
  472.6 13.5 %all-reduce = (f32[1,384]{1,0:T(1,128)S(1)}, f32[96]{0:T(128)S(1)}) all-reduce(f32[1,384]{1,0:T(1,128)S(1)} %reduce_sum.64, f32[96]{0:T(128)S(1)} %exponential_reduce_fusion.2), channel_id=1, replica_groups=mesh['wa'=4,'vert'=8] {'vert'}, use_global_device_ids=true, to_apply=%region_14.15 | all-reduce | flops 480 | bytes 3840 | tf_op jit(solution)/shard_map/psum | solution.py:12
  486.2 1.9 subtract_multiply_fusion
  488.1 3.5 copy.24
  491.7 58.5 %reduce-scatter.15.cloned.1.call-done = f32[96,2000]{1,0:T(8,128)} async-done(((f32[384,2000]{1,0:T(8,128)}), f32[96,2000]{1,0:T(8,128)}) %reduce-scatter.15.cloned.1.call-update) | async-done | bytes 768016
  552.0 11.9 %pmax.23 = f32[96]{0:T(128)S(1)} all-reduce(f32[96]{0:T(128)S(1)} %get-tuple-element.12), channel_id=1, replica_groups=mesh['wa'=4,'vert'=8] {'vert'}, use_global_device_ids=true, to_apply=%region_17.18 | all-reduce | flops 96 | bytes 768 | tf_op jit(solution)/shard_map/pmax | solution.py:11
  564.2 13.5 %psum.46 = f32[96]{0:T(128)S(1)} all-reduce(f32[96]{0:T(128)S(1)} %exponential_reduce_fusion.1), channel_id=1, replica_groups=mesh['wa'=4,'vert'=8] {'vert'}, use_global_device_ids=true, to_apply=%region_19.20 | all-reduce | flops 96 | bytes 768 | tf_op jit(solution)/shard_map/psum | solution.py:12
  579.2 12.3 %psum.47 = f32[96]{0:T(128)} all-reduce(f32[96]{0:T(128)S(1)} %get-tuple-element.10), channel_id=1, replica_groups=mesh['wa'=4,'vert'=8] {'vert'}, use_global_device_ids=true, to_apply=%region_21.22 | all-reduce | flops 96 | bytes 768 | tf_op jit(solution)/shard_map/psum | solution.py:75
  (54 shorter events, 10.0 us)
Async XLA Ops:
  7.2 110.5 %reduce-scatter.11.cloned.1.call-start = ((), (), s32[]{:S(2)}) async-start(), calls=%async_computation.5 | async-start | bytes 6881280 | tf_op jit(solution)/shard_map/reduce_scatter | solution.py:41
  18.3 1.4 copy-start.3
  18.3 200.2 %reduce-scatter.9.cloned.1.call-start = ((), (), s32[]{:S(2)}) async-start(), calls=%async_computation.4 | async-start | bytes 6881280 | tf_op jit(solution)/shard_map/reduce_scatter | solution.py:40
  31.3 187.2 %copy-start.4 = (f32[3584]{0:T(1024)S(1)}, f32[3584]{0:T(1024)}, u32[]{:S(2)}) copy-start(f32[3584]{0:T(1024)} %param.18) | copy-start | bytes 43012
  31.3 187.2 %copy-start.5 = (f32[3584]{0:T(1024)S(1)}, f32[3584]{0:T(1024)}, u32[]{:S(2)}) copy-start(f32[3584]{0:T(1024)} %param.17) | copy-start | bytes 43012
  31.3 245.6 %all-gather.3.cloned.1.call-start = ((), (), s32[]{:S(2)}) async-start(), calls=%async_computation.6 | async-start | bytes 3440640 | tf_op jit(solution)/shard_map/all_gather | solution.py:47
  221.5 136.7 %all-reduce.4.cloned.1.call-start = ((), (), s32[]{:S(2)}) async-start(), calls=%async_computation.7 | async-start | bytes 6291456 | tf_op jit(solution)/shard_map/psum | solution.py:51
  287.9 70.3 %copy-start.6 = (f32[2048]{0:T(1024)S(1)}, f32[2048]{0:T(1024)}, u32[]{:S(2)}) copy-start(f32[2048]{0:T(1024)} %param.20) | copy-start | bytes 24580
  287.9 80.3 %copy-start.10 = (f32[2048]{0:T(1024)S(1)}, f32[2048]{0:T(1024)}, u32[]{:S(2)}) copy-start(f32[2048]{0:T(1024)} %param.21) | copy-start | bytes 24580
  288.0 105.5 %all-gather.5.cloned.1.call-start = ((), (), s32[]{:S(2)}) async-start(), calls=%async_computation.8 | async-start | bytes 3538944 | tf_op jit(solution)/shard_map/all_gather | solution.py:55
  288.5 166.4 %reduce-scatter.13.cloned.1.call-start = ((), (), s32[]{:S(2)}) async-start(), calls=%async_computation.9 | async-start | bytes 3932160
  358.3 10.0 %copy-start.2 = (f32[384,2048]{1,0:T(8,128)S(1)}, f32[384,2048]{1,0:T(8,128)}, u32[]{:S(2)}) copy-start(f32[384,2048]{1,0:T(8,128)} %all-reduce.4.cloned.1.call-done) | copy-start | bytes 9437188
  377.4 0.7 copy-start.7
  377.4 18.8 %copy-start.9 = (f32[1,4096]{1,0:T(1,128)S(1)}, f32[1,4096]{1,0:T(1,128)}, u32[]{:S(2)}) copy-start(f32[1,4096]{1,0:T(1,128)} %param.24) | copy-start | bytes 49156
  377.4 172.8 %reduce-scatter.15.cloned.1.call-start = ((), (), s32[]{:S(2)}) async-start(), calls=%async_computation.10 | async-start | bytes 3932160
  393.4 2.8 copy-start.1
  491.6 60.1 %copy-start = (f32[96,2000]{0,1:T(8,128)S(1)}, f32[96,2000]{0,1:T(8,128)}, u32[]{:S(2)}) copy-start(f32[96,2000]{0,1:T(8,128)} %copy.23) | copy-start | bytes 2304004
  491.6 86.0 %copy-start.8 = (s32[96]{0:T(128)S(1)}, s32[96]{0:T(128)}, u32[]{:S(2)}) copy-start(s32[96]{0:T(128)} %param.27) | copy-start | bytes 1156
Sparse Core Ops, SparseCore 0:
  18.5 99.1 reduce-scatter.10
  119.9 98.5 reduce-scatter.8
  221.6 55.1 all-gather.2
  288.1 70.1 all-reduce.3
  360.0 33.3 all-gather.4
  395.6 59.2 reduce-scatter.12
  491.8 58.3 reduce-scatter.14
where the time goes:
time: 601 us; the launch traced here: 598 us
  waiting for transfers between devices  433 us (72%)
  blocking collectives  70 us (12%)
  matrix products  54.8 us (9%)
  other arithmetic  15.1 us (3%)
  between operations  14.2 us (2%)
  local copies, waits for them, and re-layouts  10.5 us (2%)
    unnamed x9, waiting for transfers between devices  106 us
    reduce_scatter x1, waiting for transfers between devices, local(): lax.psum_scatter(gate_part, 'wa', scatter_dimension=0, tiled=True)  101 us
    reduce_scatter x1, waiting for transfers between devices, local(): lax.psum_scatter(up_part, 'wa', scatter_dimension=0, tiled=True)  86.3 us
    psum x1, waiting for transfers between devices, local(): down = lax.psum(down_part, 'vert') * down_scale  69.7 us
    all_gather x1, waiting for transfers between devices, local(): lax.all_gather(hidden_share, 'wa', axis=0, tiled=True)  55.3 us
    psum x2, blocking collectives, log_total(): total = lax.psum(jnp.sum(jnp.exp(values - top[..., None]), axis=-1), 'vert')  27 us
    pmax x2, blocking collectives, log_total(): top = lax.pmax(local_top, 'vert')  23.8 us
    all_gather x1, waiting for transfers between devices, local(): states = lax.all_gather(reward_states, 'vert', axis=2, tiled=True)  15.4 us
  transfers between devices with their start and end apart: 7, of which 7 were waited for; matrix products, arithmetic and copies ran while one was open for 6% of the time, Pallas kernels for 0%

commit v1 on v0

v1 whole, which is shorter than its diff:
```python
import functools

import jax
import jax.numpy as jnp
from jax import lax
from jax.experimental import pallas as pl
from jax.experimental.pallas import tpu as pltpu
from jax.sharding import PartitionSpec as P

MESH = pl.DeviceIdType.MESH
VMEM = pl.BlockSpec(memory_space=pltpu.VMEM)
ANY = pl.BlockSpec(memory_space=pl.ANY)
LAG = 2
LIMIT = 60 * 2**20


def greet(n, nv):
    i, v = lax.axis_index("wa"), lax.axis_index("vert")
    barrier = pltpu.get_barrier_semaphore()
    for k in range(1, n):
        pl.semaphore_signal(
            barrier, inc=1, device_id={"wa": lax.rem(i + k, n)}, device_id_type=MESH
        )

    def one(k, carry):
        pl.semaphore_signal(
            barrier, inc=1, device_id={"vert": lax.rem(v + k, nv)}, device_id_type=MESH
        )
        return carry

    lax.fori_loop(1, nv, one, 0)
    pl.semaphore_wait(barrier, n - 1 + nv - 1)


def remote(src, dst, send, recv, axis, peer):
    return pltpu.make_async_remote_copy(
        src_ref=src,
        dst_ref=dst,
        send_sem=send,
        recv_sem=recv,
        device_id={axis: peer},
        device_id_type=MESH,
    )


def each(count, body):
    def one(k, carry):
        body(k)
        return carry

    lax.fori_loop(1, count, one, 0)


def mlp_kernel(
    n, nv, chunks, width,
    x_ref, gate_hbm, up_hbm, gate_scale, up_scale, states_ref,
    hid_ref, all_states,
    weights, own, came, going, wsem, rsend, rrecv, hsend, hrecv, ssend, srecv,
):
    i, v = lax.axis_index("wa"), lax.axis_index("vert")
    half = own.shape[2]
    span = states_ref.shape[1]
    greet(n, nv)

    def place(d):
        return all_states.at[:, pl.ds(pl.multiple_of(d * span, span), span)]

    def states_copy(k):
        return remote(
            states_ref, place(v), ssend.at[k], srecv.at[k], "vert", lax.rem(v + k, nv)
        )

    each(nv, lambda k: states_copy(k).start())

    def load(c):
        cols = pl.ds(pl.multiple_of(c * width, width), width)
        slot = lax.rem(c, 2)
        return (
            pltpu.make_async_copy(gate_hbm.at[:, cols], weights.at[slot, 0], wsem.at[slot, 0]),
            pltpu.make_async_copy(up_hbm.at[:, cols], weights.at[slot, 1], wsem.at[slot, 1]),
        )

    for copy in load(0):
        copy.start()
    all_states[:, pl.ds(pl.multiple_of(v * span, span), span)] = states_ref[...]

    def sum_copy(h, c):
        step = 1 if h else -1
        return remote(
            going.at[h, c], came.at[h, c], rsend.at[h, c], rrecv.at[h, c],
            "wa", jnp.clip(i + step, 0, n - 1),
        )

    def hidden_copy(h, c):
        step = -1 if h else 1
        view = hid_ref.at[h, :, pl.ds(pl.multiple_of(c * width, width), width)]
        return remote(
            view, view, hsend.at[h, c], hrecv.at[h, c],
            "wa", jnp.clip(i + step, 0, n - 1),
        )

    def step(s, carry):
        @pl.when(s < chunks)
        def _():
            @pl.when(s + 1 < chunks)
            def _():
                for copy in load(s + 1):
                    copy.start()

            for copy in load(s):
                copy.wait()
            slot = lax.rem(s, 2)
            for m in range(2):
                out = jnp.dot(x_ref[...], weights[slot, m], preferred_element_type=jnp.float32)
                own[s, 0, :, m * width : (m + 1) * width] = out[:half]
                own[s, 1, :, m * width : (m + 1) * width] = out[half:]

        for h in range(2):
            p = i if h else n - 1 - i
            c = s - LAG * p
            here = jnp.logical_and(c >= 0, c < chunks)

            @pl.when(jnp.logical_and(here, p == 0))
            def _():
                going[h, c] = own[c, h].astype(jnp.bfloat16)
                sum_copy(h, c).start()

            @pl.when(jnp.logical_and(here, jnp.logical_and(p > 0, p < n - 1)))
            def _():
                sum_copy(h, c).wait_recv()
                going[h, c] = (own[c, h] + came[h, c].astype(jnp.float32)).astype(jnp.bfloat16)
                sum_copy(h, c).start()

            @pl.when(jnp.logical_and(here, p == n - 1))
            def _():
                sum_copy(h, c).wait_recv()
                total = own[c, h] + came[h, c].astype(jnp.float32)
                gate = total[:, :width] * gate_scale[c]
                up = total[:, width:] * up_scale[c]
                value = (jax.nn.silu(gate) * up).astype(jnp.bfloat16)
                hid_ref[h, :, pl.ds(pl.multiple_of(c * width, width), width)] = value
                hidden_copy(h, c).start()

            q = n - 1 - p
            e = s - LAG * (n - 1) - LAG * q
            there = jnp.logical_and(jnp.logical_and(e >= 0, e < chunks), q > 0)

            @pl.when(there)
            def _():
                hidden_copy(h, e).wait_recv()

            @pl.when(jnp.logical_and(there, q < n - 1))
            def _():
                hidden_copy(h, e).start()

        return carry

    lax.fori_loop(0, chunks + 2 * LAG * (n - 1), step, 0)

    def finish(c, carry):
        for h in range(2):
            p = i if h else n - 1 - i

            @pl.when(p < n - 1)
            def _():
                sum_copy(h, c).wait_send()

            @pl.when(p > 0)
            def _():
                hidden_copy(h, c).wait_send()

        return carry

    lax.fori_loop(0, chunks, finish, 0)

    def states_done(k):
        states_copy(k).wait_send()
        remote(
            states_ref, place(lax.rem(v + nv - k, nv)), ssend.at[k], srecv.at[k],
            "vert", lax.rem(v + k, nv),
        ).wait_recv()

    each(nv, states_done)


def mlp(n, nv, x, gate_levels, up_levels, gate_scale, up_scale, states):
    rows, depth = x.shape
    total = gate_levels.shape[1]
    width = 256 if total % 256 == 0 and total // 256 > 8 else 128
    chunks = total // width
    half = rows // 2
    span = states.shape[1]
    sems = pltpu.SemaphoreType.DMA
    return pl.pallas_call(
        functools.partial(mlp_kernel, n, nv, chunks, width),
        out_shape=(
            jax.ShapeDtypeStruct((2, half, total), jnp.bfloat16),
            jax.ShapeDtypeStruct((rows, span * nv), jnp.bfloat16),
        ),
        in_specs=[VMEM, ANY, ANY, VMEM, VMEM, VMEM],
        out_specs=(VMEM, VMEM),
        scratch_shapes=[
            pltpu.VMEM((2, 2, depth, width), jnp.bfloat16),
            pltpu.VMEM((chunks, 2, half, 2 * width), jnp.float32),
            pltpu.VMEM((2, chunks, half, 2 * width), jnp.bfloat16),
            pltpu.VMEM((2, chunks, half, 2 * width), jnp.bfloat16),
            sems((2, 2)),
            sems((2, chunks)),
            sems((2, chunks)),
            sems((2, chunks)),
            sems((2, chunks)),
            sems((nv,)),
            sems((nv,)),
        ],
        compiler_params=pltpu.CompilerParams(
            collective_id=0, has_side_effects=True, vmem_limit_bytes=LIMIT
        ),
    )(
        x, gate_levels, up_levels,
        gate_scale.reshape(chunks, 1, width), up_scale.reshape(chunks, 1, width), states,
    )


def norm_kernel(
    n, nv, part_ref, x_ref, scale_ref, gain_ref, out_ref,
    came, squares, squares_in, dsend, drecv, qsend, qrecv, nsend, nrecv,
):
    i, v = lax.axis_index("wa"), lax.axis_index("vert")
    greet(n, nv)

    def part_copy(k):
        peer = lax.rem(v + k, nv)
        return remote(part_ref.at[peer], came.at[k], dsend.at[k], drecv.at[k], "vert", peer)

    each(nv, lambda k: part_copy(k).start())
    came[0] = part_ref[v]

    def add(k, acc):
        part_copy(k).wait_recv()
        return acc + came[k].astype(jnp.float32)

    down = lax.fori_loop(1, nv, add, came[0].astype(jnp.float32))
    resid = x_ref[v].astype(jnp.float32) + down * scale_ref[...]
    total = jnp.sum(resid * resid, axis=1, keepdims=True)
    squares[...] = jnp.broadcast_to(total, squares.shape)

    def square_copy(k):
        return remote(
            squares, squares_in.at[k], qsend.at[k], qrecv.at[k], "wa", lax.rem(i + k, n)
        )

    for k in range(1, n):
        square_copy(k).start()
    for k in range(1, n):
        square_copy(k).wait_recv()
        total = total + squares_in[k][:, :1]
    features = resid.shape[1] * n
    out_ref[v] = (resid * lax.rsqrt(total / features + 1e-05) * gain_ref[...]).astype(jnp.bfloat16)

    def norm_copy(k):
        return remote(
            out_ref.at[v], out_ref.at[v], nsend.at[k], nrecv.at[k], "vert", lax.rem(v + k, nv)
        )

    each(nv, lambda k: norm_copy(k).start())

    def done(k):
        other = lax.rem(v + nv - k, nv)
        remote(
            out_ref.at[v], out_ref.at[other], nsend.at[k], nrecv.at[k],
            "vert", lax.rem(v + k, nv),
        ).wait_recv()
        norm_copy(k).wait_send()
        part_copy(k).wait_send()

    each(nv, done)
    for k in range(1, n):
        square_copy(k).wait_send()


def norm(n, nv, part, x, scale, gain):
    rows, depth = x.shape
    block = rows // nv
    sems = pltpu.SemaphoreType.DMA
    out = pl.pallas_call(
        functools.partial(norm_kernel, n, nv),
        out_shape=jax.ShapeDtypeStruct((nv, block, depth), jnp.bfloat16),
        in_specs=[VMEM] * 4,
        out_specs=VMEM,
        scratch_shapes=[
            pltpu.VMEM((nv, block, depth), jnp.bfloat16),
            pltpu.VMEM((block, 128), jnp.float32),
            pltpu.VMEM((n, block, 128), jnp.float32),
            sems((nv,)),
            sems((nv,)),
            sems((n,)),
            sems((n,)),
            sems((nv,)),
            sems((nv,)),
        ],
        compiler_params=pltpu.CompilerParams(
            collective_id=1, has_side_effects=True, vmem_limit_bytes=LIMIT
        ),
    )(part.reshape(nv, block, depth), x.reshape(nv, block, depth), scale[None], gain[None])
    return out.reshape(rows, depth)


def mix_kernel(
    n, nv, part_ref, token_ref, out_ref, chosen_ref,
    came, stats, stats_in, msend, mrecv, tsend, trecv,
):
    i, v = lax.axis_index("wa"), lax.axis_index("vert")
    greet(n, nv)

    def part_copy(k):
        peer = lax.rem(i + k, n)
        return remote(part_ref.at[peer], came.at[k], msend.at[k], mrecv.at[k], "wa", peer)

    for k in range(1, n):
        part_copy(k).start()
    mix = part_ref[i].astype(jnp.float32)
    for k in range(1, n):
        part_copy(k).wait_recv()
        mix = mix + came[k].astype(jnp.float32)
    columns = mix.shape[1]
    top = jnp.max(mix, axis=1, keepdims=True)
    total = jnp.sum(jnp.exp(mix - top), axis=1, keepdims=True)
    index = lax.broadcasted_iota(jnp.int32, mix.shape, 1) + v * columns
    picked = jnp.sum(jnp.where(index == token_ref[...], mix, 0.0), axis=1, keepdims=True)
    out_ref[...] = mix
    lane = lax.broadcasted_iota(jnp.int32, stats.shape, 1)
    stats[...] = jnp.where(lane == 0, top, jnp.where(lane == 1, total, picked))

    def stat_copy(k):
        return remote(
            stats, stats_in.at[k], tsend.at[k], trecv.at[k], "vert", lax.rem(v + k, nv)
        )

    each(nv, lambda k: stat_copy(k).start())

    def merge(k, state):
        top, total, picked = state
        stat_copy(k).wait_recv()
        other = stats_in[k]
        new = jnp.maximum(top, other[:, 0:1])
        total = total * jnp.exp(top - new) + other[:, 1:2] * jnp.exp(other[:, 0:1] - new)
        return new, total, picked + other[:, 2:3]

    top, total, picked = lax.fori_loop(1, nv, merge, (top, total, picked))
    shift = top + jnp.log(total)
    out_ref[...] = out_ref[...] - shift
    chosen_ref[...] = picked - shift
    each(nv, lambda k: stat_copy(k).wait_send())
    for k in range(1, n):
        part_copy(k).wait_send()


def mix_rows(n, nv, part, token_ids):
    rows, columns = part.shape
    block = rows // n
    sems = pltpu.SemaphoreType.DMA
    log_probs, chosen = pl.pallas_call(
        functools.partial(mix_kernel, n, nv),
        out_shape=(
            jax.ShapeDtypeStruct((block, columns), jnp.float32),
            jax.ShapeDtypeStruct((block, 1), jnp.float32),
        ),
        in_specs=[VMEM] * 2,
        out_specs=(VMEM, VMEM),
        scratch_shapes=[
            pltpu.VMEM((n, block, columns), jnp.bfloat16),
            pltpu.VMEM((block, 128), jnp.float32),
            pltpu.VMEM((nv, block, 128), jnp.float32),
            sems((n,)),
            sems((n,)),
            sems((nv,)),
            sems((nv,)),
        ],
        compiler_params=pltpu.CompilerParams(
            collective_id=2, has_side_effects=True, vmem_limit_bytes=LIMIT
        ),
    )(part.reshape(n, block, columns), token_ids[:, None])
    return log_probs, chosen[:, 0]


def local(
    n,
    nv,
    hidden_in,
    gate_levels,
    up_levels,
    gate_scale,
    up_scale,
    down_levels,
    down_scale,
    norm_gain,
    head_weight,
    reward_states,
    reward_gain,
    reward_heads,
    preference,
    token_ids,
):
    rows = hidden_in.shape[0]
    models, _, span = reward_states.shape
    hidden, states = mlp(
        n, nv, hidden_in, gate_levels, up_levels, gate_scale, up_scale,
        jnp.swapaxes(reward_states, 0, 1).reshape(rows, models * span),
    )
    down_part = jnp.dot(
        hidden.reshape(rows, hidden.shape[2]), down_levels, preferred_element_type=jnp.float32
    ).astype(jnp.bfloat16)
    normed = norm(n, nv, down_part, hidden_in, down_scale, norm_gain)
    states = states.reshape(rows, nv, models, span).transpose(2, 0, 1, 3).reshape(models, rows, nv * span)
    state_values = states.astype(jnp.float32)
    state_scale = lax.rsqrt(jnp.mean(state_values * state_values, axis=2, keepdims=True) + 1e-05)
    reward_normed = (state_values * state_scale * reward_gain[:, None, :]).astype(jnp.bfloat16)
    reward_logits = jnp.einsum(
        "rnd,rdv->rnv", reward_normed, reward_heads, preferred_element_type=jnp.float32
    )
    weights = preference.astype(jnp.float32).T / 16.0
    weighted = jnp.sum(weights[:, :, None] * reward_logits, axis=0)
    base_part = jnp.dot(normed, head_weight, preferred_element_type=jnp.float32)
    return mix_rows(n, nv, (base_part + weighted).astype(jnp.bfloat16), token_ids)


def solution(mesh):
    return jax.shard_map(
        functools.partial(local, mesh.shape["wa"], mesh.shape["vert"]),
        mesh=mesh,
        in_specs=(
            P(None, "wa"),
            P("wa", "vert"),
            P("wa", "vert"),
            P("vert"),
            P("vert"),
            P("vert", "wa"),
            P("wa"),
            P("wa"),
            P("wa", "vert"),
            P("wa", None, "vert"),
            P("wa", None),
            P("wa", None, "vert"),
            P(None, "wa"),
            P("wa"),
        ),
        out_specs=(P("wa", "vert"), P("wa")),
        check_vma=False,
    )
```

time: 601 us -> 253 us (0.42)
  waiting for transfers between devices: 433 us -> 0 us
  Pallas kernels: 0 us -> 211 us
  blocking collectives: 70 us -> 0 us
  matrix products: 54.8 us -> 30.9 us
  between operations: 14.2 us -> 0.73 us
  other arithmetic: 15.1 us -> 2.15 us
    pallas_call x0 -> x3, Pallas kernels: none -> 211 us  [the longest x1 114 us: mlp(): pl.pallas_call(functools.partial(mlp_kernel, n, nv, chunks, width), out_s...]
    reduce_scatter x2 -> x0, waiting for transfers between devices: 187 us -> none  [the longest x1 101 us: local(): lax.psum_scatter(gate_part, 'wa', scatter_dimension=0, tiled=True)]
    unnamed x9 -> x0, waiting for transfers between devices: 106 us -> none
    all_gather x2 -> x0, waiting for transfers between devices: 70.6 us -> none  [the longest x1 55.3 us: local(): lax.all_gather(hidden_share, 'wa', axis=0, tiled=True)]
    psum x1 -> x0, waiting for transfers between devices: 69.7 us -> none  [local(): down = lax.psum(down_part, 'vert') * down_scale]
    psum x4 -> x0, blocking collectives: 46.2 us -> none  [the longest x2 27 us: log_total(): total = lax.psum(jnp.sum(jnp.exp(values - top[..., None]), axis=-1), 'vert')]
    pmax x2 -> x0, blocking collectives: 23.8 us -> none  [log_total(): top = lax.pmax(local_top, 'vert')]
    dot_general x3 -> x2, matrix products: 33.7 us -> 18.2 us  [the longest x1 10.8 us: local(): jnp.dot(hidden.reshape(rows, hidden.shape[2]), down_levels, preferred_ele...]
  transfers between devices with their start and end apart: 7 -> 0, of which waited for: 7 -> 0; matrix products, arithmetic and copies ran while one was open for 6% -> 0% of each run, Pallas kernels for 0% -> 0%
where the time goes in v1:
time: 253 us; the launch traced here: 252 us
  Pallas kernels  211 us (83%)
  matrix products  30.9 us (12%)
  local copies, waits for them, and re-layouts  7.72 us (3%)
    pallas_call x1, Pallas kernels, mlp(): pl.pallas_call(functools.partial(mlp_kernel, n, nv, chunks, width), out_s...  114 us
    pallas_call x1, Pallas kernels, norm(): pl.pallas_call(functools.partial(norm_kernel, n, nv), out_shape=jax.Shape...  49.9 us
    pallas_call x1, Pallas kernels, mix_rows(): pl.pallas_call(functools.partial(mix_kernel, n, nv), out_shape=(jax.Shape...  46.9 us
    dot_general x1, matrix products, local(): jnp.einsum('rnd,rdv->rnv', reward_normed, reward_heads, preferred_element...  12.7 us
    dot_general x1, matrix products, local(): jnp.dot(hidden.reshape(rows, hidden.shape[2]), down_levels, preferred_ele...  10.8 us
    dot_general x1, matrix products, local(): base_part = jnp.dot(normed, head_weight, preferred_element_type=jnp.float32)  7.42 us

profile of v1, /device:TPU:9, one launch (start us, length us, event | category | flops | bytes accessed | tf_op | source)
XLA Modules:
  0.0 252.5 jit_solution(16261095531024810119)
XLA Ops:
  0.6 1.3 reshape.67.gate_scale
  2.0 1.3 reshape.68.up_scale
  3.3 114.2 %shard_map.149 = (bf16[2,192,3584]{2,1,0:T(8,128)(2,1)}, bf16[384,4096]{1,0:T(8,128)(2,1)}) custom-call(bf16[384,2048]{1,0:T(8,128)(2,1)} %x_ref.1, bf16[2048,3584]{1,0:T(8,128)(2,1)} %gate_hbm.1, bf16[2048,3584]{1,0:T(8,128)(2,1)} %up_hbm.1, f32[14,1,256]{2,1,0:T(1,128)} %reshape.67.gate_scale, f32[14,1,256]{2,1,0:T(1,128)} %reshape.68.up_scale, ...), custom_call_target="tpu_custom_call" | custom-call | tf_op jit(solution)/shard_map/pallas_call | solution.py:194
  117.5 10.8 %convolution_convert_fusion = bf16[384,2048]{1,0:T(8,128)(2,1)} fusion(bf16[384,3584]{1,0:T(8,128)(2,1)} %bitcast.27, bf16[3584,2048]{1,0:T(8,128)(2,1)} %param.19), kind=kOutput, calls=%fused_computation.10 | convolution fusion | flops 5637931008 | bytes 19005440 | tf_op jit(solution)/shard_map/dot_general | solution.py:410
  128.3 49.9 %shard_map.150 = bf16[8,48,2048]{2,1,0:T(8,128)(2,1)} custom-call(bf16[8,48,2048]{2,1,0:T(8,128)(2,1)} %bitcast.21, bf16[8,48,2048]{2,1,0:T(8,128)(2,1)} %bitcast.19, f32[1,2048]{1,0:T(1,128)} %bitcast.24, f32[1,2048]{1,0:T(1,128)} %bitcast.25), custom_call_target="tpu_custom_call" | custom-call | tf_op jit(solution)/shard_map/pallas_call | solution.py:285
  178.2 0.0 copy-start
  178.2 7.4 %fusion.12 = f32[384,2000]{0,1:T(8,128)S(1)} fusion(bf16[384,2048]{1,0:T(8,128)(2,1)} %bitcast.22, bf16[2048,2000]{0,1:T(8,128)(2,1)} %param.22), kind=kOutput, calls=%fused_computation.13 | convolution fusion | flops 3145728000 | bytes 12836864 | tf_op jit(solution)/shard_map/dot_general | solution.py:423
  185.7 0.0 copy-start.1
  185.7 0.0 copy-start.3
  185.7 0.0 copy-done
  185.7 0.7 fusion.2
  186.4 0.0 copy-done.1
  186.4 0.0 copy-done.3
  186.4 0.0 copy-start.2
  186.5 12.7 %add_convert_fusion = bf16[384,2000]{0,1:T(8,128)(2,1)S(1)} fusion(f32[384,2000]{0,1:T(8,128)S(1)} %fusion.12, bf16[1,4096,2000]{1,2,0:T(8,128)(2,1)} %param.25, bf16[384,4096]{1,0:T(8,128)(2,1)S(1)} %copy-done, f32[4096]{0:T(1024)S(1)} %bitcast.28, f32[384]{0:T(512)S(1)} %add_rsqrt_fusion, f32[384]{0:T(512)S(1)} %multiply_reduce_fusion), kind=kOutput, calls=%fused_computation.9 | convolution fusion | flops 6300051456 | bytes 24157184 | tf_op jit(solution)/shard_map/rnd,rdv->rnv/dot_general | solution.py:418
  199.1 2.3 copy.18
  201.4 0.0 copy-done.2
  201.4 0.7 copy.19.token_ref
  202.1 46.9 %shard_map.151 = (f32[96,2000]{1,0:T(8,128)}, f32[96,1]{1,0:T(8,128)}) custom-call(bf16[4,96,2000]{2,1,0:T(8,128)(2,1)} %bitcast.20, s32[96,1]{1,0:T(8,128)} %copy.19.token_ref), custom_call_target="tpu_custom_call" | custom-call | tf_op jit(solution)/shard_map/pallas_call | solution.py:362
  249.0 1.4 reduce.3
  250.4 2.1 copy.21
  (2 shorter events, 0.0 us)
Async XLA Ops:
  178.2 7.5 %copy-start = (bf16[384,4096]{1,0:T(8,128)(2,1)S(1)}, bf16[384,4096]{1,0:T(8,128)(2,1)}, u32[]{:S(2)}) copy-start(bf16[384,4096]{1,0:T(8,128)(2,1)} %get-tuple-element.7) | copy-start | bytes 9437188
  185.7 0.7 copy-start.1
  185.7 0.8 copy-start.3
  186.4 14.9 %copy-start.2 = (s32[96]{0:T(128)S(1)}, s32[96]{0:T(128)}, u32[]{:S(2)}) copy-start(s32[96]{0:T(128)} %param.27) | copy-start | bytes 1156
